TPU v7x, 32 devices: a whole 2x2x4 slice. The times are simulated.
32 devices in a mesh: groups: 2 (over y), chan: 4 (over z), tm: 2 (over x), sub: 2 (over core).
Axes of the slice: x: 2, y: 2, z: 4, core: 2. Of those that a mesh axis runs over, the one named last changes fastest.
Arguments:
- traces: float32 [2048, 8192], P(('groups', 'chan', 'sub'), 'tm'), parts along dimension 0, may hold values from -6 to 6
- filters: float32 [2048, 65], P(('groups', 'chan', 'sub')), parts along dimension 0, may hold values from -0.75 to 0.75
- sources: int32 [256], P('groups'), parts along dimension 0, may hold values from 0 to 1023, as said below
Outputs:
- corr: float32 [128, 129, 2048], P('tm', None, ('groups', 'chan', 'sub')), parts along dimension 2
There are 2 independent parts, one for each index of `groups`. A program takes and returns all parts, laid end to end along the dimension named above; each array names one. Nothing has to cross between parts.
Inputs may be any that keep to these rules, and one draw needn't show every extreme that they name: `sources`: the 128 partner channels are distinct. No block of 128 consecutive channels starting at a multiple of 128 holds more than 16 of them, and some block holds exactly 16.
All inputs are finite; a program needn't handle non-finite values.
Results may differ from a plain program's by a relative error of at most 0.0033.
Values may be sent and summed in bfloat16 or wider, within the bound.
A program may use at most 64 MiB of HBM per device.

v0:
```python
import functools
import math

import jax
import jax.numpy as jnp
from jax import lax
from jax.experimental import pallas as pl
from jax.experimental.pallas import tpu as pltpu
from jax.sharding import PartitionSpec as P

LAGS = 129
HALF = 64
EDGE = 128
LANES = 128
TB = 128
VMEM_LIMIT = 60 * 1024 * 1024


def filtered(xt, start, f_ref, taps):
    acc = jnp.zeros((TB, xt.shape[1]), jnp.float32)
    for r in range(8):
        part = None
        for m in range((taps - 1 - r) // 8 + 1):
            k = 8 * m + r
            term = f_ref[k : k + 1, :] * xt[pl.ds(start + 8 * m, TB + 8), :]
            part = term if part is None else part + term
        acc = acc + part[r : r + TB]
    return acc


def whiten_kernel(taps, x_ref, low_ref, high_ref, f_ref, pick_ref, w_ref, slot_ref, xt):
    seg = x_ref.shape[1]
    half_taps = (taps - 1) // 2
    lead = EDGE - half_taps
    xt[0:EDGE, :] = low_ref[...].T
    xt[seg + EDGE : seg + 2 * EDGE, :] = high_ref[...].T

    @pl.loop(0, seg // LANES)
    def _(b):
        t0 = pl.multiple_of(b * LANES, LANES)
        xt[pl.ds(t0 + EDGE, LANES), :] = x_ref[:, pl.ds(t0, LANES)].T

    @pl.loop(0, seg // TB)
    def _(b):
        t0 = pl.multiple_of(b * TB, TB)
        w = filtered(xt, t0 + lead, f_ref, taps).astype(jnp.bfloat16)
        w_ref[pl.ds(t0, TB), :] = w
        slot_ref[:, pl.ds(t0, TB)] = lax.dot_general(
            pick_ref[...], w, (((1,), (1,)), ((), ())), preferred_element_type=jnp.float32
        ).astype(jnp.bfloat16)


def whiten(x, low, high, filters_t, picker):
    chans, seg = x.shape
    slots = picker.shape[0]
    return pl.pallas_call(
        functools.partial(whiten_kernel, filters_t.shape[0]),
        out_shape=(
            jax.ShapeDtypeStruct((seg, chans), jnp.bfloat16),
            jax.ShapeDtypeStruct((slots, seg), jnp.bfloat16),
        ),
        in_specs=[pl.BlockSpec(memory_space=pltpu.VMEM)] * 5,
        out_specs=(pl.BlockSpec(memory_space=pltpu.VMEM),) * 2,
        scratch_shapes=[pltpu.VMEM((seg + 2 * EDGE, chans), jnp.float32)],
        compiler_params=pltpu.CompilerParams(vmem_limit_bytes=VMEM_LIMIT),
        name="whiten",
    )(x, low, high, filters_t, picker)


MESH = pl.DeviceIdType.MESH
CHUNKS = 4


def front_kernel(taps, sizes, x_ref, f_ref, pick_ref, w_ref, slot_ref, xt, low, high,
                 halo_send, halo_recv, w_send, w_recv, slot_send, slot_recv):
    peers, lines, subs = sizes
    seg = x_ref.shape[1]
    width = seg // CHUNKS
    half_taps = (taps - 1) // 2
    lead = EDGE - half_taps
    a, z, s = lax.axis_index("tm"), lax.axis_index("chan"), lax.axis_index("sub")
    other = lax.rem(a + 1, peers)
    twin = lax.rem(s + 1, subs)

    barrier = pltpu.get_barrier_semaphore()
    pl.semaphore_signal(barrier, inc=1, device_id={"tm": other}, device_id_type=MESH)
    pl.semaphore_signal(barrier, inc=1, device_id={"sub": twin}, device_id_type=MESH)
    for step in range(1, lines):
        pl.semaphore_signal(
            barrier, inc=1, device_id={"chan": lax.rem(z + step, lines)}, device_id_type=MESH
        )
    pl.semaphore_wait(barrier, lines + 1)

    def halo(side):
        src = x_ref.at[:, seg - EDGE : seg] if side == 0 else x_ref.at[:, 0:EDGE]
        return pltpu.make_async_remote_copy(
            src_ref=src, dst_ref=(low, high)[side], send_sem=halo_send.at[side],
            recv_sem=halo_recv.at[side], device_id={"tm": other}, device_id_type=MESH)

    halo(0).start()
    halo(1).start()

    def w_copy(q, part):
        view = w_ref.at[part, q * width : (q + 1) * width, :]
        return pltpu.make_async_remote_copy(
            src_ref=view, dst_ref=view, send_sem=w_send.at[q], recv_sem=w_recv.at[q],
            device_id={"tm": other}, device_id_type=MESH)

    def slot_copy(q, part, line, sub, lane, where):
        view = slot_ref.at[part, line, sub, :, q * width : (q + 1) * width]
        return pltpu.make_async_remote_copy(
            src_ref=view, dst_ref=view, send_sem=slot_send.at[q, lane],
            recv_sem=slot_recv.at[q, part, line, sub], device_id=where, device_id_type=MESH)

    def others():
        return [lax.rem(z + step, lines) for step in range(1, lines)]

    def spread(q, part, base):
        copies = [
            slot_copy(q, part, z, s, base + i, {"chan": line}) for i, line in enumerate(others())
        ]
        return copies + [slot_copy(q, part, z, s, base + lines - 1, {"sub": twin})]

    def first(q):
        return [slot_copy(q, a, z, s, 0, {"tm": other})] + spread(q, a, 1)

    def second(q):
        return spread(q, other, 1 + lines)

    def third(q):
        return [
            slot_copy(q, part, line, s, 1 + 2 * lines + i * (lines - 1) + j, {"sub": twin})
            for i, part in enumerate((a, other))
            for j, line in enumerate(others())
        ]

    def launch(copies):
        for copy in copies:
            copy.start()

    def stage_two(q):
        slot_copy(q, other, z, s, 0, {"tm": other}).wait_recv()
        launch(second(q))

    def stage_three(q):
        for part in (a, other):
            for line in others():
                slot_copy(q, part, line, s, 0, {"chan": line}).wait_recv()
        launch(third(q))

    @pl.loop(0, seg // LANES)
    def _(b):
        t0 = pl.multiple_of(b * LANES, LANES)
        xt[pl.ds(t0 + EDGE, LANES), :] = x_ref[:, pl.ds(t0, LANES)].T

    halo(0).wait_recv()
    halo(1).wait_recv()
    xt[0:EDGE, :] = jnp.where(a > 0, low[...], 0.0).T
    xt[seg + EDGE : seg + 2 * EDGE, :] = jnp.where(a < peers - 1, high[...], 0.0).T

    for q in range(CHUNKS):

        @pl.loop(0, width // TB)
        def _(b):
            t0 = pl.multiple_of(q * width + b * TB, TB)
            w_ref[a, pl.ds(t0, TB), :] = filtered(xt, t0 + lead, f_ref, taps).astype(jnp.bfloat16)

        slot_ref[a, z, s, :, q * width : (q + 1) * width] = lax.dot_general(
            pick_ref[...], w_ref[a, q * width : (q + 1) * width, :],
            (((1,), (1,)), ((), ())), preferred_element_type=jnp.float32,
        ).astype(jnp.bfloat16)
        launch(first(q))
        w_copy(q, a).start()
        if q >= 1:
            stage_two(q - 1)
        if q >= 2:
            stage_three(q - 2)
    stage_two(CHUNKS - 1)
    stage_three(CHUNKS - 2)
    stage_three(CHUNKS - 1)
    halo(0).wait_send()
    halo(1).wait_send()
    for q in range(CHUNKS):
        for part in (a, other):
            for line in [z] + others():
                slot_copy(q, part, line, twin, 0, {"sub": twin}).wait_recv()
        w_copy(q, other).wait_recv()
        w_copy(q, a).wait_send()
        for copy in first(q) + second(q) + third(q):
            copy.wait_send()


def front(x, filters_t, picker, sizes):
    chans, seg = x.shape
    peers, lines, subs = sizes
    slots = picker.shape[0]
    dma = pltpu.SemaphoreType.DMA
    return pl.pallas_call(
        functools.partial(front_kernel, filters_t.shape[0], sizes),
        out_shape=(
            jax.ShapeDtypeStruct((peers, seg, chans), jnp.bfloat16),
            jax.ShapeDtypeStruct((peers, lines, subs, slots, seg), jnp.bfloat16),
        ),
        in_specs=[pl.BlockSpec(memory_space=pltpu.VMEM)] * 3,
        out_specs=(pl.BlockSpec(memory_space=pltpu.VMEM),) * 2,
        scratch_shapes=[
            pltpu.VMEM((seg + 2 * EDGE, chans), jnp.float32),
            pltpu.VMEM((chans, EDGE), jnp.float32),
            pltpu.VMEM((chans, EDGE), jnp.float32),
            dma((2,)), dma((2,)), dma((CHUNKS,)), dma((CHUNKS,)),
            dma((CHUNKS, 1 + 2 * lines + 2 * (lines - 1))),
            dma((CHUNKS, peers, lines, subs)),
        ],
        compiler_params=pltpu.CompilerParams(
            vmem_limit_bytes=VMEM_LIMIT, collective_id=0, has_side_effects=True
        ),
        name="front",
    )(x, filters_t, picker)


def chunk_of(total):
    return max(d for d in range(256, 1025, 256) if total % d == 0)


GROUP = 13


def corr_kernel(scale, w_ref, slot_ref, sel_ref, out_ref, rhs, xp, acc):
    parts, seg, chans = w_ref.shape
    span = parts * seg
    rows = sel_ref.shape[0]
    total = rhs.shape[0]
    depth = chunk_of(total)
    rhs[span:total, 0:chans] = jnp.zeros((total - span, chans), jnp.bfloat16)
    rhs[0:HALF, chans:] = jnp.zeros((HALF, chans), jnp.bfloat16)
    rhs[span + HALF : total, chans:] = jnp.zeros((total - span - HALF, chans), jnp.bfloat16)
    xp[:, 0:EDGE] = jnp.zeros((rows, EDGE), jnp.bfloat16)
    xp[:, EDGE + span :] = jnp.zeros((rows, xp.shape[1] - EDGE - span), jnp.bfloat16)
    for part in range(parts):
        rhs[part * seg : (part + 1) * seg, 0:chans] = w_ref[part]
        rhs[HALF + part * seg : HALF + (part + 1) * seg, chans:] = w_ref[part]
        xp[:, EDGE + part * seg : EDGE + (part + 1) * seg] = jnp.dot(
            sel_ref[...], slot_ref[part], preferred_element_type=jnp.float32
        ).astype(jnp.bfloat16)
    acc[...] = jnp.zeros_like(acc)

    @pl.loop(0, total // depth)
    def _(kb):
        k0 = pl.multiple_of(kb * depth, 256)
        xw = xp[:, pl.ds(k0, depth + 128)]
        r = rhs[pl.ds(k0, depth), :]
        for g in range((HALF + 1) // GROUP):
            lhs = jnp.concatenate(
                [
                    pltpu.roll(xw, depth + LANES - HALF - i, 1)[:, :depth]
                    for i in range(g * GROUP, (g + 1) * GROUP)
                ],
                axis=0,
            )
            here = slice(g * GROUP * rows, (g + 1) * GROUP * rows)
            acc[here, :] += jnp.dot(lhs, r, preferred_element_type=jnp.float32)

    for i in range(HALF + 1):
        if i < HALF:
            out_ref[i] = acc[i * rows : (i + 1) * rows, 0:chans] * scale
        out_ref[i + HALF] = acc[i * rows : (i + 1) * rows, chans:] * scale


def correlate(w_full, slots, select, scale):
    parts, seg, chans = w_full.shape
    rows = select.shape[0]
    total = parts * seg + 256
    return pl.pallas_call(
        functools.partial(corr_kernel, scale),
        out_shape=jax.ShapeDtypeStruct((LAGS, rows, chans), jnp.float32),
        in_specs=[pl.BlockSpec(memory_space=pltpu.VMEM)] * 3,
        out_specs=pl.BlockSpec(memory_space=pltpu.VMEM),
        scratch_shapes=[
            pltpu.VMEM((total, 2 * chans), jnp.bfloat16),
            pltpu.VMEM((rows, total + 128), jnp.bfloat16),
            pltpu.VMEM(((HALF + 1) * rows, 2 * chans), jnp.float32),
        ],
        compiler_params=pltpu.CompilerParams(vmem_limit_bytes=VMEM_LIMIT),
        name="correlate",
    )(w_full, slots, select)


def routing(sources, chan_dev, wide):
    partner_count = sources.shape[0]
    my_block = lax.axis_index(("chan", "sub"))
    owners = sources // chan_dev
    within = sources % chan_dev
    is_mine = owners == my_block
    chan_ids = jnp.arange(wide, dtype=jnp.int32)
    slot_most = min(chan_dev, partner_count // 8)
    order_ids = jnp.arange(partner_count, dtype=jnp.int32)
    same_owner = owners[:, None] == owners[None, :]
    earlier = order_ids[None, :] < order_ids[:, None]
    rank_in = jnp.sum((same_owner & earlier).astype(jnp.int32), axis=1)
    choose = (
        (rank_in[None, :] == jnp.arange(slot_most, dtype=jnp.int32)[:, None]) & is_mine[None, :]
    ).astype(jnp.bfloat16)
    onehot = (within[:, None] == chan_ids[None, :]).astype(jnp.bfloat16)
    picker = jnp.dot(choose, onehot, preferred_element_type=jnp.float32).astype(jnp.bfloat16)
    return picker, owners * slot_most + rank_in


def on_device(traces, filters, sources):
    chan_dev, seg_len = traces.shape
    time_devs = lax.axis_size("tm")
    wide = -(-chan_dev // LANES) * LANES
    picker, slot_id = routing(sources, chan_dev, wide)
    if wide != chan_dev:
        traces = jnp.pad(traces, ((0, wide - chan_dev), (0, 0)))
        filters = jnp.pad(filters, ((0, wide - chan_dev), (0, 0)))
    rows = slot_id.shape[0] // time_devs
    mine = lax.dynamic_slice_in_dim(slot_id, lax.axis_index("tm") * rows, rows, 0)
    lines, subs = lax.axis_size("chan"), lax.axis_size("sub")
    slot_count = picker.shape[0] * lines * subs
    select = (mine[:, None] == jnp.arange(slot_count, dtype=jnp.int32)[None, :]).astype(jnp.bfloat16)
    scale = 1.0 / math.sqrt(seg_len * time_devs)
    if time_devs == 2 and subs == 2:
        w_full, slots = front(traces, filters.T, picker, (time_devs, lines, subs))
        slots = slots.reshape(time_devs, slot_count, seg_len)
        corr = correlate(w_full, slots, select, scale)
    else:
        forward = [(i, i + 1) for i in range(time_devs - 1)]
        backward = [(target, source) for source, target in forward]
        low = lax.ppermute(traces[:, seg_len - EDGE :], "tm", forward)
        high = lax.ppermute(traces[:, :EDGE], "tm", backward)
        w_t, slot_rows = whiten(traces, low, high, filters.T, picker)
        segment = lax.all_gather(slot_rows, ("chan", "sub"), axis=0, tiled=True)
        w_full = lax.all_gather(w_t, "tm", axis=0, tiled=True)
        every = (
            slot_id[:, None] == jnp.arange(slot_count, dtype=jnp.int32)[None, :]
        ).astype(jnp.bfloat16)
        partners = jnp.dot(every, segment, preferred_element_type=jnp.float32).astype(jnp.bfloat16)
        partners = lax.all_to_all(partners, "tm", split_axis=0, concat_axis=1, tiled=True)
        corr = correlate(
            w_full[None], partners[None], jnp.eye(rows, dtype=jnp.bfloat16), scale
        )
    return jnp.transpose(corr, (1, 0, 2))[:, :, :chan_dev]


def solution(mesh):
    return jax.shard_map(
        on_device,
        mesh=mesh,
        in_specs=(
            P(("groups", "chan", "sub"), "tm"),
            P(("groups", "chan", "sub"), None),
            P("groups"),
        ),
        out_specs=P("tm", None, ("groups", "chan", "sub")),
        check_vma=False,
    )
```

profile of v0, /device:TPU:0, one launch (start us, length us, event | category | flops | bytes accessed | tf_op | source)
XLA Modules:
  0.0 76.9 jit_solution(16302192251123750982)
XLA Ops:
  0.0 0.7 and_select_fusion
  0.7 0.7 broadcast_compare_fusion
  1.3 0.2 convert_reduce_fusion
  1.5 0.1 dynamic_slice.3
  1.6 0.8 %convolution_convert_fusion.pick_ref = bf16[16,128]{1,0:T(8,128)(2,1)} fusion(s32[128]{0:T(128)S(1)} %and_select_fusion, s32[128]{0:T(128)S(1)} %convert_reduce_fusion, pred[128]{0:T(512)(128)(4,1)S(1)} %get-tuple-element.9), kind=kOutput, calls=%fused_computation | convolution fusion | flops 546816 | bytes 5248 | tf_op jit(solution)/shard_map/dot_general | solution.py:304
  2.4 0.7 fusion.2.sel_ref
  3.1 43.7 %front.1 = (bf16[2,4096,128]{2,1,0:T(8,128)(2,1)}, bf16[2,4,2,16,4096]{4,3,2,1,0:T(8,128)(2,1)}) custom-call(f32[128,4096]{1,0:T(8,128)} %x_ref.1, f32[65,128]{1,0:T(8,128)} %bitcast.4, bf16[16,128]{1,0:T(8,128)(2,1)} %convolution_convert_fusion.pick_ref), custom_call_target="tpu_custom_call" | custom-call | tf_op jit(solution)/shard_map/front/pallas_call | solution.py:198
  46.7 30.2 %correlate.1 = f32[129,64,128]{2,1,0:T(8,128)} custom-call(bf16[2,4096,128]{2,1,0:T(8,128)(2,1)} %get-tuple-element.7.w_ref, bf16[2,128,4096]{2,1,0:T(8,128)(2,1)} %bitcast.3, bf16[64,128]{1,0:T(8,128)(2,1)} %fusion.2.sel_ref), custom_call_target="tpu_custom_call" | custom-call | tf_op jit(solution)/shard_map/correlate/pallas_call | solution.py:273
  (1 shorter events, 0.0 us)
where the time goes:
time: 77.1 us; the launch traced here: 76.9 us
  Pallas kernels  73.8 us (96%)
  other arithmetic  2.17 us (3%)
  matrix products  0.8 us (1%)
    pallas_call x1, Pallas kernels, front(): pl.pallas_call(functools.partial(front_kernel, filters_t.shape[0], sizes)...  43.7 us
    pallas_call x1, Pallas kernels, correlate(): pl.pallas_call(functools.partial(corr_kernel, scale), out_shape=jax.Shape...  30.2 us

commit v1 on v0

--- a/solution.py
+++ b/solution.py
@@ -13,7 +13,7 @@
 EDGE = 128
 LANES = 128
 TB = 128
-VMEM_LIMIT = 60 * 1024 * 1024
+VMEM_LIMIT = 26 * 1024 * 1024
 
 
 def filtered(xt, start, f_ref, taps):

time: 77.1 us -> 72.5 us (0.940)
  Pallas kernels: 73.8 us -> 68 us
  local copies, waits for them, and re-layouts: 0.08 us -> 2.44 us
    pallas_call x1, Pallas kernels: 43.7 us -> 40.1 us  [front(): pl.pallas_call(functools.partial(front_kernel, filters_t.shape[0], sizes)...]
    unnamed x0 -> x4, local copies, waits for them, and re-layouts: none -> 2.36 us
    pallas_call x1, Pallas kernels: 30.2 us -> 27.9 us  [correlate(): pl.pallas_call(functools.partial(corr_kernel, scale), out_shape=jax.Shape...]
where the time goes in v1:
time: 72.5 us; the launch traced here: 72.3 us
  Pallas kernels  68 us (94%)
  local copies, waits for them, and re-layouts  2.44 us (3%)
  other arithmetic  1.58 us (2%)
    pallas_call x1, Pallas kernels, front(): pl.pallas_call(functools.partial(front_kernel, filters_t.shape[0], sizes)...  40.1 us
    pallas_call x1, Pallas kernels, correlate(): pl.pallas_call(functools.partial(corr_kernel, scale), out_shape=jax.Shape...  27.9 us
    unnamed x4, local copies, waits for them, and re-layouts  2.36 us

profile of v1, /device:TPU:0, one launch (start us, length us, event | category | flops | bytes accessed | tf_op | source)
XLA Modules:
  0.0 72.3 jit_solution(9411357718575196270)
XLA Ops:
  0.0 0.7 and_select_fusion
  0.7 0.7 broadcast_compare_fusion
  1.3 0.2 convert_reduce_fusion
  1.5 0.1 dynamic_slice.3
  1.6 0.2 convolution_convert_fusion.pick_ref
  1.8 0.1 fusion.2.sel_ref
  1.9 0.0 copy-start
  1.9 1.6 %copy-done = f32[128,4096]{1,0:T(8,128)S(1)} copy-done((f32[128,4096]{1,0:T(8,128)S(1)}, f32[128,4096]{1,0:T(8,128)}, u32[]{:S(2)}) %copy-start) | copy-done | bytes 2097176
  3.5 0.0 copy-start.1
  3.5 0.8 %copy-done.1 = f32[128,65]{0,1:T(8,128)S(1)} copy-done((f32[128,65]{0,1:T(8,128)S(1)}, f32[128,65]{0,1:T(8,128)}, u32[]{:S(2)}) %copy-start.1) | copy-done | bytes 33304
  4.2 40.1 %front.1 = (bf16[2,4096,128]{2,1,0:T(8,128)(2,1)S(1)}, bf16[2,4,2,16,4096]{4,3,2,1,0:T(8,128)(2,1)S(1)}) custom-call(f32[128,4096]{1,0:T(8,128)S(1)} %copy-done, f32[65,128]{1,0:T(8,128)S(1)} %bitcast.4, bf16[16,128]{1,0:T(8,128)(2,1)S(1)} %convolution_convert_fusion.pick_ref), custom_call_target="tpu_custom_call" | custom-call | tf_op jit(solution)/shard_map/front/pallas_call | solution.py:198
  44.4 27.9 %correlate.1 = f32[129,64,128]{2,1,0:T(8,128)} custom-call(bf16[2,4096,128]{2,1,0:T(8,128)(2,1)S(1)} %get-tuple-element.7.w_ref, bf16[2,128,4096]{2,1,0:T(8,128)(2,1)S(1)} %bitcast.3, bf16[64,128]{1,0:T(8,128)(2,1)S(1)} %fusion.2.sel_ref), custom_call_target="tpu_custom_call" | custom-call | tf_op jit(solution)/shard_map/correlate/pallas_call | solution.py:273
  (1 shorter events, 0.0 us)
Async XLA Ops:
  1.9 1.6 %copy-start = (f32[128,4096]{1,0:T(8,128)S(1)}, f32[128,4096]{1,0:T(8,128)}, u32[]{:S(2)}) copy-start(f32[128,4096]{1,0:T(8,128)} %x_ref.1) | copy-start | bytes 6291460
  3.5 0.8 %copy-start.1 = (f32[128,65]{0,1:T(8,128)S(1)}, f32[128,65]{0,1:T(8,128)}, u32[]{:S(2)}) copy-start(f32[128,65]{0,1:T(8,128)} %param.4) | copy-start | bytes 99844

commit v2 on v0

--- a/solution.py
+++ b/solution.py
@@ -69,12 +69,79 @@
 
 MESH = pl.DeviceIdType.MESH
 CHUNKS = 4
-
-
-def front_kernel(taps, sizes, x_ref, f_ref, pick_ref, w_ref, slot_ref, xt, low, high,
-                 halo_send, halo_recv, w_send, w_recv, slot_send, slot_recv):
+DEEP = 1024
+GROUP = 13
+FRONT_LIMIT = 26 * 1024 * 1024
+REST_LIMIT = 16 * 1024 * 1024
+
+
+def accumulated(w_ref, xp_ref, k0, depth, chosen):
+    xw = xp_ref[:, pl.ds(k0, depth + LANES)]
+    r = jnp.concatenate(
+        [
+            w_ref[pl.ds(pl.multiple_of(k0 + EDGE, EDGE), depth), :],
+            w_ref[pl.ds(pl.multiple_of(k0 + EDGE - HALF, HALF), depth), :],
+        ],
+        axis=1,
+    )
+    for group in chosen:
+        lhs = jnp.concatenate(
+            [pltpu.roll(xw, depth + LANES - HALF - i, 1)[:, :depth] for i in group], axis=0
+        )
+        yield group, jnp.dot(lhs, r, preferred_element_type=jnp.float32)
+
+
+def groups():
+    return [range(g, g + GROUP) for g in range(0, HALF + 1, GROUP)]
+
+
+def add_terms(w_ref, xp_ref, acc_ref, k0, depth):
+    rows = xp_ref.shape[0]
+    for group, term in accumulated(w_ref, xp_ref, k0, depth, groups()):
+        acc_ref[group[0] * rows : (group[-1] + 1) * rows, :] += term
+
+
+def routing_tables(src, block, rows, half, blocks, chan_dev, slot_most, wide):
+    count = src.shape[1]
+    across = jnp.broadcast_to(src, (count, count))
+    down = across.T
+
+    def owner_of(ids):
+        owner = jnp.zeros(ids.shape, jnp.int32)
+        for b in range(1, blocks):
+            owner = owner + jnp.where(ids >= b * chan_dev, 1, 0)
+        return owner
+
+    own_across, own_down = owner_of(across), owner_of(down)
+    p_down = lax.broadcasted_iota(jnp.int32, (count, count), 0)
+    p_across = lax.broadcasted_iota(jnp.int32, (count, count), 1)
+    same = own_across == own_down
+    rank_down = jnp.sum(jnp.where(same & (p_across < p_down), 1.0, 0.0), axis=1, keepdims=True)
+    rank_across = jnp.sum(jnp.where(same & (p_down < p_across), 1.0, 0.0), axis=0, keepdims=True)
+    slot_ids = lax.broadcasted_iota(jnp.int32, (slot_most, count), 0).astype(jnp.float32)
+    mine = own_across[0:slot_most] == block
+    choose = jnp.where((slot_ids == rank_across) & mine, 1.0, 0.0).astype(jnp.bfloat16)
+    chan_ids = lax.broadcasted_iota(jnp.int32, (count, wide), 1)
+    within = down[:, 0:1] - own_down[:, 0:1] * chan_dev
+    onehot = jnp.where(within == chan_ids, 1.0, 0.0).astype(jnp.bfloat16)
+    picker = jnp.dot(choose, onehot, preferred_element_type=jnp.float32).astype(jnp.bfloat16)
+    slot_down = own_down[:, 0:1].astype(jnp.float32) * slot_most + rank_down
+    slot_count = blocks * slot_most
+    slots = lax.broadcasted_iota(jnp.int32, (count, slot_count), 1).astype(jnp.float32)
+    every = jnp.where(slot_down == slots, 1.0, 0.0)
+    select = every[0:rows]
+    for h in range(1, count // rows):
+        select = jnp.where(half == h, every[h * rows : (h + 1) * rows], select)
+    return picker, select.astype(jnp.bfloat16)
+
+
+def front_kernel(taps, sizes, slot_most, x_ref, f_ref, src_ref, w_ref, xp_ref, acc_ref,
+                 x_v, xt, low, high, slot_ref, pick_ref, sel_ref,
+                 x_sem, halo_send, halo_recv, w_send, w_recv, slot_send, slot_recv):
     peers, lines, subs = sizes
-    seg = x_ref.shape[1]
+    chans, seg = x_ref.shape
+    span = peers * seg
+    rows = xp_ref.shape[0]
     width = seg // CHUNKS
     half_taps = (taps - 1) // 2
     lead = EDGE - half_taps
@@ -89,6 +156,25 @@
         pl.semaphore_signal(
             barrier, inc=1, device_id={"chan": lax.rem(z + step, lines)}, device_id_type=MESH
         )
+
+    def x_copy(q):
+        here = slice(q * width, (q + 1) * width)
+        return pltpu.make_async_copy(x_ref.at[:, here], x_v.at[:, here], x_sem.at[q])
+
+    for q in range(CHUNKS):
+        x_copy(q).start()
+
+    picker, select = routing_tables(
+        src_ref[...], z * subs + s, rows, a, lines * subs, chans, slot_most, chans
+    )
+    pick_ref[...] = picker
+    sel_ref[...] = select
+    w_ref[0:EDGE, :] = jnp.zeros((EDGE, chans), jnp.bfloat16)
+    w_ref[EDGE + span :, :] = jnp.zeros((w_ref.shape[0] - EDGE - span, chans), jnp.bfloat16)
+    xp_ref[:, 0:EDGE] = jnp.zeros((rows, EDGE), jnp.bfloat16)
+    xp_ref[:, EDGE + span :] = jnp.zeros((rows, xp_ref.shape[1] - EDGE - span), jnp.bfloat16)
+    acc_ref[...] = jnp.zeros_like(acc_ref)
+
     pl.semaphore_wait(barrier, lines + 1)
 
     def halo(side):
@@ -100,14 +186,20 @@
     halo(0).start()
     halo(1).start()
 
+    def place(part, q):
+        return pl.multiple_of(EDGE + part * seg + q * width, EDGE)
+
     def w_copy(q, part):
-        view = w_ref.at[part, q * width : (q + 1) * width, :]
+        view = w_ref.at[pl.ds(place(part, q), width), :]
         return pltpu.make_async_remote_copy(
             src_ref=view, dst_ref=view, send_sem=w_send.at[q], recv_sem=w_recv.at[q],
             device_id={"tm": other}, device_id_type=MESH)
 
+    def columns(q):
+        return pl.ds(pl.multiple_of(q * width, LANES), width)
+
     def slot_copy(q, part, line, sub, lane, where):
-        view = slot_ref.at[part, line, sub, :, q * width : (q + 1) * width]
+        view = slot_ref.at[part, line, sub, :, columns(q)]
         return pltpu.make_async_remote_copy(
             src_ref=view, dst_ref=view, send_sem=slot_send.at[q, lane],
             recv_sem=slot_recv.at[q, part, line, sub], device_id=where, device_id_type=MESH)
@@ -127,10 +219,10 @@
     def second(q):
         return spread(q, other, 1 + lines)
 
-    def third(q):
+    def third(q, part):
+        base = 1 + 2 * lines + (0 if part is a else lines - 1)
         return [
-            slot_copy(q, part, line, s, 1 + 2 * lines + i * (lines - 1) + j, {"sub": twin})
-            for i, part in enumerate((a, other))
+            slot_copy(q, part, line, s, base + j, {"sub": twin})
             for j, line in enumerate(others())
         ]
 
@@ -138,91 +230,191 @@
         for copy in copies:
             copy.start()
 
-    def stage_two(q):
+    def across_time(q):
         slot_copy(q, other, z, s, 0, {"tm": other}).wait_recv()
         launch(second(q))
 
-    def stage_three(q):
-        for part in (a, other):
-            for line in others():
-                slot_copy(q, part, line, s, 0, {"chan": line}).wait_recv()
-        launch(third(q))
-
-    @pl.loop(0, seg // LANES)
-    def _(b):
-        t0 = pl.multiple_of(b * LANES, LANES)
-        xt[pl.ds(t0 + EDGE, LANES), :] = x_ref[:, pl.ds(t0, LANES)].T
-
-    halo(0).wait_recv()
-    halo(1).wait_recv()
-    xt[0:EDGE, :] = jnp.where(a > 0, low[...], 0.0).T
-    xt[seg + EDGE : seg + 2 * EDGE, :] = jnp.where(a < peers - 1, high[...], 0.0).T
+    def to_twin(q, part):
+        for line in others():
+            slot_copy(q, part, line, s, 0, {"chan": line}).wait_recv()
+        launch(third(q, part))
+
+    def fill_partners(q, part):
+        for line in [z] + others():
+            slot_copy(q, part, line, twin, 0, {"sub": twin}).wait_recv()
+        rows_in = slot_ref[part, :, :, :, columns(q)].reshape(-1, width)
+        xp_ref[:, pl.ds(place(part, q), width)] = jnp.dot(
+            sel_ref[...], rows_in, preferred_element_type=jnp.float32
+        ).astype(jnp.bfloat16)
+
+    def nth(j):
+        return lax.rem(j + 1, CHUNKS)
 
     for q in range(CHUNKS):
+        x_copy(q).wait()
+
+        @pl.loop(0, width // LANES)
+        def _(b):
+            t0 = pl.multiple_of(q * width + b * LANES, LANES)
+            xt[pl.ds(t0 + EDGE, LANES), :] = x_v[:, pl.ds(t0, LANES)].T
+
+    @pl.loop(0, CHUNKS)
+    def _(j):
+        q = nth(j)
+
+        @pl.when(j == CHUNKS - 2)
+        def _():
+            halo(0).wait_recv()
+            halo(1).wait_recv()
+            xt[0:EDGE, :] = jnp.where(a > 0, low[...], 0.0).T
+            xt[seg + EDGE : seg + 2 * EDGE, :] = jnp.where(a < peers - 1, high[...], 0.0).T
 
         @pl.loop(0, width // TB)
         def _(b):
             t0 = pl.multiple_of(q * width + b * TB, TB)
-            w_ref[a, pl.ds(t0, TB), :] = filtered(xt, t0 + lead, f_ref, taps).astype(jnp.bfloat16)
-
-        slot_ref[a, z, s, :, q * width : (q + 1) * width] = lax.dot_general(
-            pick_ref[...], w_ref[a, q * width : (q + 1) * width, :],
+            w_ref[pl.ds(pl.multiple_of(EDGE + a * seg + t0, TB), TB), :] = filtered(
+                xt, t0 + lead, f_ref, taps
+            ).astype(jnp.bfloat16)
+
+        slot_ref[a, z, s, :, columns(q)] = lax.dot_general(
+            pick_ref[...], w_ref[pl.ds(place(a, q), width), :],
             (((1,), (1,)), ((), ())), preferred_element_type=jnp.float32,
         ).astype(jnp.bfloat16)
         launch(first(q))
         w_copy(q, a).start()
-        if q >= 1:
-            stage_two(q - 1)
-        if q >= 2:
-            stage_three(q - 2)
-    stage_two(CHUNKS - 1)
-    stage_three(CHUNKS - 2)
-    stage_three(CHUNKS - 1)
+
+        @pl.when(j >= 1)
+        def _():
+            to_twin(nth(j - 1), a)
+
+    @pl.loop(0, CHUNKS - 1)
+    def _(j):
+        fill_partners(nth(j), a)
+
+    near = a * (seg + 256)
+
+    @pl.loop(0, CHUNKS)
+    def _(j):
+        deep = jnp.where(j < CHUNKS - 2, j + 2, CHUNKS - 1 - j)
+        add_terms(w_ref, xp_ref, acc_ref, pl.multiple_of(near + deep * width, 256), width)
+        across_time(nth(j))
+
+        @pl.when(j == 0)
+        def _():
+            to_twin(nth(CHUNKS - 1), a)
+
+        @pl.when(j == CHUNKS - 3)
+        def _():
+            fill_partners(nth(CHUNKS - 1), a)
+
+        @pl.when(j >= 1)
+        def _():
+            to_twin(nth(j - 1), other)
+
+    to_twin(nth(CHUNKS - 1), other)
     halo(0).wait_send()
     halo(1).wait_send()
-    for q in range(CHUNKS):
-        for part in (a, other):
-            for line in [z] + others():
-                slot_copy(q, part, line, twin, 0, {"sub": twin}).wait_recv()
+
+    @pl.loop(0, CHUNKS)
+    def _(j):
+        q = nth(j)
+        fill_partners(q, other)
         w_copy(q, other).wait_recv()
         w_copy(q, a).wait_send()
-        for copy in first(q) + second(q) + third(q):
+        for copy in first(q) + second(q) + third(q, a) + third(q, other):
             copy.wait_send()
 
 
-def front(x, filters_t, picker, sizes):
+def front(x, filters_t, sources, sizes, slot_most):
     chans, seg = x.shape
     peers, lines, subs = sizes
-    slots = picker.shape[0]
+    rows = sources.shape[0] // peers
+    total = peers * seg + 256
     dma = pltpu.SemaphoreType.DMA
+    vmem = pl.BlockSpec(memory_space=pltpu.VMEM)
     return pl.pallas_call(
-        functools.partial(front_kernel, filters_t.shape[0], sizes),
+        functools.partial(front_kernel, filters_t.shape[0], sizes, slot_most),
         out_shape=(
-            jax.ShapeDtypeStruct((peers, seg, chans), jnp.bfloat16),
-            jax.ShapeDtypeStruct((peers, lines, subs, slots, seg), jnp.bfloat16),
+            jax.ShapeDtypeStruct((total + EDGE, chans), jnp.bfloat16),
+            jax.ShapeDtypeStruct((rows, total + LANES), jnp.bfloat16),
+            jax.ShapeDtypeStruct(((HALF + 1) * rows, 2 * chans), jnp.float32),
         ),
-        in_specs=[pl.BlockSpec(memory_space=pltpu.VMEM)] * 3,
-        out_specs=(pl.BlockSpec(memory_space=pltpu.VMEM),) * 2,
+        in_specs=[pl.BlockSpec(memory_space=pl.ANY), vmem, vmem],
+        out_specs=(vmem,) * 3,
         scratch_shapes=[
+            pltpu.VMEM((chans, seg), jnp.float32),
             pltpu.VMEM((seg + 2 * EDGE, chans), jnp.float32),
             pltpu.VMEM((chans, EDGE), jnp.float32),
             pltpu.VMEM((chans, EDGE), jnp.float32),
-            dma((2,)), dma((2,)), dma((CHUNKS,)), dma((CHUNKS,)),
+            pltpu.VMEM((peers, lines, subs, slot_most, seg), jnp.bfloat16),
+            pltpu.VMEM((slot_most, chans), jnp.bfloat16),
+            pltpu.VMEM((rows, lines * subs * slot_most), jnp.bfloat16),
+            dma((CHUNKS,)), dma((2,)), dma((2,)), dma((CHUNKS,)), dma((CHUNKS,)),
             dma((CHUNKS, 1 + 2 * lines + 2 * (lines - 1))),
             dma((CHUNKS, peers, lines, subs)),
         ],
         compiler_params=pltpu.CompilerParams(
-            vmem_limit_bytes=VMEM_LIMIT, collective_id=0, has_side_effects=True
+            vmem_limit_bytes=FRONT_LIMIT, collective_id=0, has_side_effects=True
         ),
         name="front",
-    )(x, filters_t, picker)
+    )(x, filters_t, sources.reshape(1, -1))
+
+
+def rest_kernel(scale, seg, w_ref, xp_ref, acc_ref, out_ref, part, stage, sems):
+    rows = xp_ref.shape[0]
+    chans = w_ref.shape[1]
+    far = (1 - lax.axis_index("tm")) * seg
+    for group, term in accumulated(w_ref, xp_ref, pl.multiple_of(far, 256), 256, groups()):
+        here = slice(group[0] * rows, (group[-1] + 1) * rows)
+        part[here, :] = acc_ref[here, :] + term
+
+    @pl.loop(0, seg // DEEP - 1)
+    def _(b):
+        add_terms(w_ref, xp_ref, part, pl.multiple_of(far + 256 + b * DEEP, 256), DEEP)
+
+    last = pl.multiple_of(far + 256 + seg - DEEP, 256)
+    copies = []
+    for n, (group, term) in enumerate(accumulated(w_ref, xp_ref, last, DEEP, groups())):
+        start = group[0]
+        for i in group:
+            here = slice((i - start) * rows, (i - start + 1) * rows)
+            held = part[i * rows : (i + 1) * rows, :] + term[here]
+            if i < HALF:
+                stage[i] = held[:, 0:chans] * scale
+            stage[i + HALF] = held[:, chans:] * scale
+        for m, (low, high) in enumerate(
+            ((start, min(group[-1] + 1, HALF)), (start + HALF, group[-1] + 1 + HALF))
+        ):
+            copy = pltpu.make_async_copy(
+                stage.at[low:high], out_ref.at[low:high], sems.at[n, m]
+            )
+            copy.start()
+            copies.append(copy)
+    for copy in copies:
+        copy.wait()
+
+
+def rest(w_full, partners, terms, seg, scale):
+    rows = partners.shape[0]
+    chans = w_full.shape[1]
+    vmem = pl.BlockSpec(memory_space=pltpu.VMEM)
+    return pl.pallas_call(
+        functools.partial(rest_kernel, scale, seg),
+        out_shape=jax.ShapeDtypeStruct((LAGS, rows, chans), jnp.float32),
+        in_specs=[vmem] * 3,
+        out_specs=pl.BlockSpec(memory_space=pl.ANY),
+        scratch_shapes=[
+            pltpu.VMEM(terms.shape, jnp.float32),
+            pltpu.VMEM((LAGS, rows, chans), jnp.float32),
+            pltpu.SemaphoreType.DMA((len(groups()), 2)),
+        ],
+        compiler_params=pltpu.CompilerParams(vmem_limit_bytes=REST_LIMIT),
+        name="rest",
+    )(w_full, partners, terms)
 
 
 def chunk_of(total):
     return max(d for d in range(256, 1025, 256) if total % d == 0)
-
-
-GROUP = 13
 
 
 def corr_kernel(scale, w_ref, slot_ref, sel_ref, out_ref, rhs, xp, acc):
@@ -308,37 +500,36 @@
 def on_device(traces, filters, sources):
     chan_dev, seg_len = traces.shape
     time_devs = lax.axis_size("tm")
+    lines, subs = lax.axis_size("chan"), lax.axis_size("sub")
+    scale = 1.0 / math.sqrt(seg_len * time_devs)
+    if time_devs == 2 and subs == 2 and chan_dev == LANES and seg_len % (CHUNKS * DEEP) == 0:
+        slot_most = min(chan_dev, sources.shape[0] // 8)
+        w_full, partners, terms = front(
+            traces, filters.T, sources, (time_devs, lines, subs), slot_most
+        )
+        return jnp.transpose(rest(w_full, partners, terms, seg_len, scale), (1, 0, 2))
     wide = -(-chan_dev // LANES) * LANES
     picker, slot_id = routing(sources, chan_dev, wide)
     if wide != chan_dev:
         traces = jnp.pad(traces, ((0, wide - chan_dev), (0, 0)))
         filters = jnp.pad(filters, ((0, wide - chan_dev), (0, 0)))
     rows = slot_id.shape[0] // time_devs
-    mine = lax.dynamic_slice_in_dim(slot_id, lax.axis_index("tm") * rows, rows, 0)
-    lines, subs = lax.axis_size("chan"), lax.axis_size("sub")
     slot_count = picker.shape[0] * lines * subs
-    select = (mine[:, None] == jnp.arange(slot_count, dtype=jnp.int32)[None, :]).astype(jnp.bfloat16)
-    scale = 1.0 / math.sqrt(seg_len * time_devs)
-    if time_devs == 2 and subs == 2:
-        w_full, slots = front(traces, filters.T, picker, (time_devs, lines, subs))
-        slots = slots.reshape(time_devs, slot_count, seg_len)
-        corr = correlate(w_full, slots, select, scale)
-    else:
-        forward = [(i, i + 1) for i in range(time_devs - 1)]
-        backward = [(target, source) for source, target in forward]
-        low = lax.ppermute(traces[:, seg_len - EDGE :], "tm", forward)
-        high = lax.ppermute(traces[:, :EDGE], "tm", backward)
-        w_t, slot_rows = whiten(traces, low, high, filters.T, picker)
-        segment = lax.all_gather(slot_rows, ("chan", "sub"), axis=0, tiled=True)
-        w_full = lax.all_gather(w_t, "tm", axis=0, tiled=True)
-        every = (
-            slot_id[:, None] == jnp.arange(slot_count, dtype=jnp.int32)[None, :]
-        ).astype(jnp.bfloat16)
-        partners = jnp.dot(every, segment, preferred_element_type=jnp.float32).astype(jnp.bfloat16)
-        partners = lax.all_to_all(partners, "tm", split_axis=0, concat_axis=1, tiled=True)
-        corr = correlate(
-            w_full[None], partners[None], jnp.eye(rows, dtype=jnp.bfloat16), scale
-        )
+    forward = [(i, i + 1) for i in range(time_devs - 1)]
+    backward = [(target, source) for source, target in forward]
+    low = lax.ppermute(traces[:, seg_len - EDGE :], "tm", forward)
+    high = lax.ppermute(traces[:, :EDGE], "tm", backward)
+    w_t, slot_rows = whiten(traces, low, high, filters.T, picker)
+    segment = lax.all_gather(slot_rows, ("chan", "sub"), axis=0, tiled=True)
+    w_full = lax.all_gather(w_t, "tm", axis=0, tiled=True)
+    every = (
+        slot_id[:, None] == jnp.arange(slot_count, dtype=jnp.int32)[None, :]
+    ).astype(jnp.bfloat16)
+    partners = jnp.dot(every, segment, preferred_element_type=jnp.float32).astype(jnp.bfloat16)
+    partners = lax.all_to_all(partners, "tm", split_axis=0, concat_axis=1, tiled=True)
+    corr = correlate(
+        w_full[None], partners[None], jnp.eye(rows, dtype=jnp.bfloat16), scale
+    )
     return jnp.transpose(corr, (1, 0, 2))[:, :, :chan_dev]
 
 

time: 77.1 us -> 59.8 us (0.78)
  Pallas kernels: 73.8 us -> 56.5 us
  local copies, waits for them, and re-layouts: 0.08 us -> 3.01 us
  other arithmetic: 2.17 us -> 0 us
  matrix products: 0.8 us -> 0 us
    pallas_call x2, Pallas kernels: 73.8 us -> 56.5 us  [the longest x1 43.4 us: front(): pl.pallas_call(functools.partial(front_kernel, filters_t.shape[0], sizes,...]
    unnamed x0 -> x6, local copies, waits for them, and re-layouts: none -> 3.01 us
    dot_general x1 -> x0, matrix products: 0.8 us -> none  [routing(): jnp.dot(choose, onehot, preferred_element_type=jnp.float32)]
where the time goes in v2:
time: 59.8 us; the launch traced here: 59.6 us
  Pallas kernels  56.5 us (94%)
  local copies, waits for them, and re-layouts  3.01 us (5%)
    pallas_call x1, Pallas kernels, front(): pl.pallas_call(functools.partial(front_kernel, filters_t.shape[0], sizes,...  43.4 us
    pallas_call x1, Pallas kernels, rest(): pl.pallas_call(functools.partial(rest_kernel, scale, seg), out_shape=jax....  13.2 us
    unnamed x6, local copies, waits for them, and re-layouts  3.01 us

profile of v2, /device:TPU:0, one launch (start us, length us, event | category | flops | bytes accessed | tf_op | source)
XLA Modules:
  0.0 59.6 jit_solution(7345965932342175081)
XLA Ops:
  0.0 0.0 copy-start
  0.0 1.6 %copy-done = f32[128,4096]{1,0:T(8,128)S(1)} copy-done((f32[128,4096]{1,0:T(8,128)S(1)}, f32[128,4096]{1,0:T(8,128)}, u32[]{:S(2)}) %copy-start) | copy-done | bytes 2097176
  1.6 0.0 copy-start.1
  1.6 0.8 %copy-done.1 = f32[128,65]{0,1:T(8,128)S(1)} copy-done((f32[128,65]{0,1:T(8,128)S(1)}, f32[128,65]{0,1:T(8,128)}, u32[]{:S(2)}) %copy-start.1) | copy-done | bytes 33304
  2.4 0.0 copy-start.2
  2.4 0.7 %copy-done.2 = s32[128]{0:T(128)S(1)} copy-done((s32[128]{0:T(128)S(1)}, s32[128]{0:T(128)}, u32[]{:S(2)}) %copy-start.2) | copy-done | bytes 536
  3.0 43.4 %front.1 = (bf16[8576,128]{1,0:T(8,128)(2,1)S(1)}, bf16[64,8576]{1,0:T(8,128)(2,1)S(1)}, f32[4160,256]{1,0:T(8,128)S(1)}) custom-call(f32[128,4096]{1,0:T(8,128)S(1)} %copy-done, f32[65,128]{1,0:T(8,128)S(1)} %bitcast.3, s32[1,128]{1,0:T(1,128)S(1)} %bitcast.4), custom_call_target="tpu_custom_call" | custom-call | tf_op jit(solution)/shard_map/front/pallas_call | solution.py:335
  46.4 13.2 %rest.1 = f32[129,64,128]{2,1,0:T(8,128)} custom-call(bf16[8576,128]{1,0:T(8,128)(2,1)S(1)} %get-tuple-element.8.w_ref, bf16[64,8576]{1,0:T(8,128)(2,1)S(1)} %get-tuple-element.9.xp_ref, f32[4160,256]{1,0:T(8,128)S(1)} %get-tuple-element.10.acc_ref), custom_call_target="tpu_custom_call" | custom-call | tf_op jit(solution)/shard_map/rest/pallas_call | solution.py:401
Async XLA Ops:
  0.0 1.6 %copy-start = (f32[128,4096]{1,0:T(8,128)S(1)}, f32[128,4096]{1,0:T(8,128)}, u32[]{:S(2)}) copy-start(f32[128,4096]{1,0:T(8,128)} %x_ref.1) | copy-start | bytes 6291460
  1.6 0.8 %copy-start.1 = (f32[128,65]{0,1:T(8,128)S(1)}, f32[128,65]{0,1:T(8,128)}, u32[]{:S(2)}) copy-start(f32[128,65]{0,1:T(8,128)} %param.4) | copy-start | bytes 99844
  2.4 0.7 %copy-start.2 = (s32[128]{0:T(128)S(1)}, s32[128]{0:T(128)}, u32[]{:S(2)}) copy-start(s32[128]{0:T(128)} %param.5) | copy-start | bytes 1540

commit v3 on v2

--- a/solution.py
+++ b/solution.py
@@ -69,7 +69,6 @@
 
 MESH = pl.DeviceIdType.MESH
 CHUNKS = 4
-DEEP = 1024
 GROUP = 13
 FRONT_LIMIT = 26 * 1024 * 1024
 REST_LIMIT = 16 * 1024 * 1024
@@ -135,9 +134,9 @@
     return picker, select.astype(jnp.bfloat16)
 
 
-def front_kernel(taps, sizes, slot_most, x_ref, f_ref, src_ref, w_ref, xp_ref, acc_ref,
-                 x_v, xt, low, high, slot_ref, pick_ref, sel_ref,
-                 x_sem, halo_send, halo_recv, w_send, w_recv, slot_send, slot_recv):
+def front_kernel(taps, sizes, slot_most, x_ref, f_hbm, src_hbm, w_ref, xp_ref, acc_ref,
+                 f_ref, src_ref, x_v, xt, low, high, slot_ref, pick_ref, sel_ref,
+                 x_sem, in_sem, halo_send, halo_recv, w_send, w_recv, slot_send, slot_recv):
     peers, lines, subs = sizes
     chans, seg = x_ref.shape
     span = peers * seg
@@ -161,19 +160,27 @@
         here = slice(q * width, (q + 1) * width)
         return pltpu.make_async_copy(x_ref.at[:, here], x_v.at[:, here], x_sem.at[q])
 
+    small = [
+        pltpu.make_async_copy(src_hbm, src_ref, in_sem.at[0]),
+        pltpu.make_async_copy(f_hbm, f_ref, in_sem.at[1]),
+    ]
+    for copy in small:
+        copy.start()
     for q in range(CHUNKS):
         x_copy(q).start()
+    w_ref[0:EDGE, :] = jnp.zeros((EDGE, chans), jnp.bfloat16)
+    w_ref[EDGE + span :, :] = jnp.zeros((w_ref.shape[0] - EDGE - span, chans), jnp.bfloat16)
+    xp_ref[:, 0:EDGE] = jnp.zeros((rows, EDGE), jnp.bfloat16)
+    xp_ref[:, EDGE + span :] = jnp.zeros((rows, xp_ref.shape[1] - EDGE - span), jnp.bfloat16)
+    acc_ref[...] = jnp.zeros_like(acc_ref)
+    for copy in small:
+        copy.wait()
 
     picker, select = routing_tables(
         src_ref[...], z * subs + s, rows, a, lines * subs, chans, slot_most, chans
     )
     pick_ref[...] = picker
     sel_ref[...] = select
-    w_ref[0:EDGE, :] = jnp.zeros((EDGE, chans), jnp.bfloat16)
-    w_ref[EDGE + span :, :] = jnp.zeros((w_ref.shape[0] - EDGE - span, chans), jnp.bfloat16)
-    xp_ref[:, 0:EDGE] = jnp.zeros((rows, EDGE), jnp.bfloat16)
-    xp_ref[:, EDGE + span :] = jnp.zeros((rows, xp_ref.shape[1] - EDGE - span), jnp.bfloat16)
-    acc_ref[...] = jnp.zeros_like(acc_ref)
 
     pl.semaphore_wait(barrier, lines + 1)
 
@@ -247,8 +254,10 @@
             sel_ref[...], rows_in, preferred_element_type=jnp.float32
         ).astype(jnp.bfloat16)
 
+    final = CHUNKS - 1
+
     def nth(j):
-        return lax.rem(j + 1, CHUNKS)
+        return jnp.where(j >= final, j, lax.rem(j + 1, final))
 
     for q in range(CHUNKS):
         x_copy(q).wait()
@@ -281,7 +290,14 @@
             (((1,), (1,)), ((), ())), preferred_element_type=jnp.float32,
         ).astype(jnp.bfloat16)
         launch(first(q))
-        w_copy(q, a).start()
+
+        @pl.when((j == 0) | (j == final))
+        def _():
+            w_copy(nth(jnp.where(j == 0, 0, final - 1)), a).start()
+
+        @pl.when(j >= 2)
+        def _():
+            w_copy(nth(jnp.where(j == final, final, j - 1)), a).start()
 
         @pl.when(j >= 1)
         def _():
@@ -292,34 +308,56 @@
         fill_partners(nth(j), a)
 
     near = a * (seg + 256)
+    far = other * seg
+
+    def add_chunk(base, q):
+        add_terms(w_ref, xp_ref, acc_ref, pl.multiple_of(base + q * width, 256), width)
 
     @pl.loop(0, CHUNKS)
     def _(j):
-        deep = jnp.where(j < CHUNKS - 2, j + 2, CHUNKS - 1 - j)
-        add_terms(w_ref, xp_ref, acc_ref, pl.multiple_of(near + deep * width, 256), width)
-        across_time(nth(j))
+        add_chunk(near, jnp.where(j < 2, 1 - j, j))
 
         @pl.when(j == 0)
         def _():
-            to_twin(nth(CHUNKS - 1), a)
-
-        @pl.when(j == CHUNKS - 3)
-        def _():
-            fill_partners(nth(CHUNKS - 1), a)
+            across_time(nth(0))
+            to_twin(nth(final), a)
+
+        @pl.when(j < final)
+        def _():
+            across_time(nth(j + 1))
+
+        @pl.when(j == 1)
+        def _():
+            fill_partners(nth(final), a)
 
         @pl.when(j >= 1)
         def _():
             to_twin(nth(j - 1), other)
 
-    to_twin(nth(CHUNKS - 1), other)
+    to_twin(nth(final), other)
+
+    def arrive(j):
+        q = nth(j)
+        fill_partners(q, other)
+        w_copy(q, other).wait_recv()
+
+    arrive(0)
+
+    @pl.loop(1, CHUNKS)
+    def _(j):
+        @pl.when(j < final)
+        def _():
+            arrive(j)
+
+        add_chunk(far, CHUNKS - 1 - j)
+
+    arrive(final)
     halo(0).wait_send()
     halo(1).wait_send()
 
     @pl.loop(0, CHUNKS)
     def _(j):
         q = nth(j)
-        fill_partners(q, other)
-        w_copy(q, other).wait_recv()
         w_copy(q, a).wait_send()
         for copy in first(q) + second(q) + third(q, a) + third(q, other):
             copy.wait_send()
@@ -339,9 +377,11 @@
             jax.ShapeDtypeStruct((rows, total + LANES), jnp.bfloat16),
             jax.ShapeDtypeStruct(((HALF + 1) * rows, 2 * chans), jnp.float32),
         ),
-        in_specs=[pl.BlockSpec(memory_space=pl.ANY), vmem, vmem],
+        in_specs=[pl.BlockSpec(memory_space=pltpu.HBM)] * 3,
         out_specs=(vmem,) * 3,
         scratch_shapes=[
+            pltpu.VMEM(filters_t.shape, jnp.float32),
+            pltpu.VMEM((1, sources.shape[0]), jnp.int32),
             pltpu.VMEM((chans, seg), jnp.float32),
             pltpu.VMEM((seg + 2 * EDGE, chans), jnp.float32),
             pltpu.VMEM((chans, EDGE), jnp.float32),
@@ -349,7 +389,7 @@
             pltpu.VMEM((peers, lines, subs, slot_most, seg), jnp.bfloat16),
             pltpu.VMEM((slot_most, chans), jnp.bfloat16),
             pltpu.VMEM((rows, lines * subs * slot_most), jnp.bfloat16),
-            dma((CHUNKS,)), dma((2,)), dma((2,)), dma((CHUNKS,)), dma((CHUNKS,)),
+            dma((CHUNKS,)), dma((2,)), dma((2,)), dma((2,)), dma((CHUNKS,)), dma((CHUNKS,)),
             dma((CHUNKS, 1 + 2 * lines + 2 * (lines - 1))),
             dma((CHUNKS, peers, lines, subs)),
         ],
@@ -357,28 +397,24 @@
             vmem_limit_bytes=FRONT_LIMIT, collective_id=0, has_side_effects=True
         ),
         name="front",
-    )(x, filters_t, sources.reshape(1, -1))
-
-
-def rest_kernel(scale, seg, w_ref, xp_ref, acc_ref, out_ref, part, stage, sems):
+    )(*(
+        pltpu.with_memory_space_constraint(value, pltpu.HBM)
+        for value in (x, filters_t, sources.reshape(1, -1))
+    ))
+
+
+def rest_kernel(scale, seg, w_ref, xp_ref, acc_ref, out_ref, stage, sems):
     rows = xp_ref.shape[0]
     chans = w_ref.shape[1]
     far = (1 - lax.axis_index("tm")) * seg
-    for group, term in accumulated(w_ref, xp_ref, pl.multiple_of(far, 256), 256, groups()):
-        here = slice(group[0] * rows, (group[-1] + 1) * rows)
-        part[here, :] = acc_ref[here, :] + term
-
-    @pl.loop(0, seg // DEEP - 1)
-    def _(b):
-        add_terms(w_ref, xp_ref, part, pl.multiple_of(far + 256 + b * DEEP, 256), DEEP)
-
-    last = pl.multiple_of(far + 256 + seg - DEEP, 256)
+    width = seg // CHUNKS
+    last = pl.multiple_of(far + seg - width, 256)
     copies = []
-    for n, (group, term) in enumerate(accumulated(w_ref, xp_ref, last, DEEP, groups())):
+    for n, (group, term) in enumerate(accumulated(w_ref, xp_ref, last, width + 256, groups())):
         start = group[0]
         for i in group:
             here = slice((i - start) * rows, (i - start + 1) * rows)
-            held = part[i * rows : (i + 1) * rows, :] + term[here]
+            held = acc_ref[i * rows : (i + 1) * rows, :] + term[here]
             if i < HALF:
                 stage[i] = held[:, 0:chans] * scale
             stage[i + HALF] = held[:, chans:] * scale
@@ -404,7 +440,6 @@
         in_specs=[vmem] * 3,
         out_specs=pl.BlockSpec(memory_space=pl.ANY),
         scratch_shapes=[
-            pltpu.VMEM(terms.shape, jnp.float32),
             pltpu.VMEM((LAGS, rows, chans), jnp.float32),
             pltpu.SemaphoreType.DMA((len(groups()), 2)),
         ],
@@ -502,7 +537,7 @@
     time_devs = lax.axis_size("tm")
     lines, subs = lax.axis_size("chan"), lax.axis_size("sub")
     scale = 1.0 / math.sqrt(seg_len * time_devs)
-    if time_devs == 2 and subs == 2 and chan_dev == LANES and seg_len % (CHUNKS * DEEP) == 0:
+    if time_devs == 2 and subs == 2 and chan_dev == LANES and seg_len % (CHUNKS * 256) == 0:
         slot_most = min(chan_dev, sources.shape[0] // 8)
         w_full, partners, terms = front(
             traces, filters.T, sources, (time_devs, lines, subs), slot_most

time: 59.8 us -> 54.4 us (0.910)
  local copies, waits for them, and re-layouts: 3.01 us -> 0 us
  Pallas kernels: 56.5 us -> 54.3 us
    pallas_call x1, Pallas kernels: 13.2 us -> 4.58 us  [rest(): pl.pallas_call(functools.partial(rest_kernel, scale, seg), out_shape=jax....]
    pallas_call x1, Pallas kernels: 43.4 us -> 49.7 us  [front(): pl.pallas_call(functools.partial(front_kernel, filters_t.shape[0], sizes,...]
    unnamed x6 -> x0, local copies, waits for them, and re-layouts: 3.01 us -> none
where the time goes in v3:
time: 54.4 us; the launch traced here: 54.3 us
  Pallas kernels  54.3 us (100%)
    pallas_call x1, Pallas kernels, front(): pl.pallas_call(functools.partial(front_kernel, filters_t.shape[0], sizes,...  49.7 us
    pallas_call x1, Pallas kernels, rest(): pl.pallas_call(functools.partial(rest_kernel, scale, seg), out_shape=jax....  4.58 us

profile of v3, /device:TPU:0, one launch (start us, length us, event | category | flops | bytes accessed | tf_op | source)
XLA Modules:
  0.0 54.3 jit_solution(3289701968111833210)
XLA Ops:
  0.0 49.7 %front.1 = (bf16[8576,128]{1,0:T(8,128)(2,1)S(1)}, bf16[64,8576]{1,0:T(8,128)(2,1)S(1)}, f32[4160,256]{1,0:T(8,128)S(1)}) custom-call(f32[128,4096]{1,0:T(8,128)} %x_ref.1, f32[65,128]{1,0:T(8,128)} %bitcast.3, s32[1,128]{1,0:T(1,128)} %bitcast.4), custom_call_target="tpu_custom_call" | custom-call | tf_op jit(solution)/shard_map/front/pallas_call | solution.py:373
  49.7 4.6 %rest.1 = f32[129,64,128]{2,1,0:T(8,128)} custom-call(bf16[8576,128]{1,0:T(8,128)(2,1)S(1)} %get-tuple-element.8.w_ref, bf16[64,8576]{1,0:T(8,128)(2,1)S(1)} %get-tuple-element.9.xp_ref, f32[4160,256]{1,0:T(8,128)S(1)} %get-tuple-element.10.acc_ref), custom_call_target="tpu_custom_call" | custom-call | tf_op jit(solution)/shard_map/rest/pallas_call | solution.py:437

commit v4 on v3

--- a/solution.py
+++ b/solution.py
@@ -182,16 +182,11 @@
     pick_ref[...] = picker
     sel_ref[...] = select
 
-    pl.semaphore_wait(barrier, lines + 1)
-
     def halo(side):
         src = x_ref.at[:, seg - EDGE : seg] if side == 0 else x_ref.at[:, 0:EDGE]
         return pltpu.make_async_remote_copy(
             src_ref=src, dst_ref=(low, high)[side], send_sem=halo_send.at[side],
             recv_sem=halo_recv.at[side], device_id={"tm": other}, device_id_type=MESH)
-
-    halo(0).start()
-    halo(1).start()
 
     def place(part, q):
         return pl.multiple_of(EDGE + part * seg + q * width, EDGE)
@@ -267,17 +262,7 @@
             t0 = pl.multiple_of(q * width + b * LANES, LANES)
             xt[pl.ds(t0 + EDGE, LANES), :] = x_v[:, pl.ds(t0, LANES)].T
 
-    @pl.loop(0, CHUNKS)
-    def _(j):
-        q = nth(j)
-
-        @pl.when(j == CHUNKS - 2)
-        def _():
-            halo(0).wait_recv()
-            halo(1).wait_recv()
-            xt[0:EDGE, :] = jnp.where(a > 0, low[...], 0.0).T
-            xt[seg + EDGE : seg + 2 * EDGE, :] = jnp.where(a < peers - 1, high[...], 0.0).T
-
+    def whiten_chunk(q):
         @pl.loop(0, width // TB)
         def _(b):
             t0 = pl.multiple_of(q * width + b * TB, TB)
@@ -289,21 +274,37 @@
             pick_ref[...], w_ref[pl.ds(place(a, q), width), :],
             (((1,), (1,)), ((), ())), preferred_element_type=jnp.float32,
         ).astype(jnp.bfloat16)
-        launch(first(q))
-
-        @pl.when((j == 0) | (j == final))
-        def _():
-            w_copy(nth(jnp.where(j == 0, 0, final - 1)), a).start()
+
+    whiten_chunk(1)
+    pl.semaphore_wait(barrier, lines + 1)
+    halo(0).start()
+    halo(1).start()
+    launch(first(1))
+    w_copy(1, a).start()
+
+    @pl.loop(1, CHUNKS)
+    def _(j):
+        @pl.when(j == CHUNKS - 2)
+        def _():
+            halo(0).wait_recv()
+            halo(1).wait_recv()
+            xt[0:EDGE, :] = jnp.where(a > 0, low[...], 0.0).T
+            xt[seg + EDGE : seg + 2 * EDGE, :] = jnp.where(a < peers - 1, high[...], 0.0).T
+
+        whiten_chunk(nth(j))
+        launch(first(nth(j)))
 
         @pl.when(j >= 2)
         def _():
-            w_copy(nth(jnp.where(j == final, final, j - 1)), a).start()
-
-        @pl.when(j >= 1)
-        def _():
-            to_twin(nth(j - 1), a)
-
-    @pl.loop(0, CHUNKS - 1)
+            w_copy(nth(j - 1), a).start()
+            to_twin(nth(j - 2), a)
+
+    w_copy(nth(final), a).start()
+    across_time(nth(0))
+    to_twin(nth(final - 1), a)
+    across_time(nth(1))
+
+    @pl.loop(0, 2)
     def _(j):
         fill_partners(nth(j), a)
 
@@ -315,26 +316,25 @@
 
     @pl.loop(0, CHUNKS)
     def _(j):
-        add_chunk(near, jnp.where(j < 2, 1 - j, j))
+        add_chunk(near, jnp.where(j < final - a, final - 1 - a - j, j))
 
         @pl.when(j == 0)
         def _():
-            across_time(nth(0))
+            fill_partners(nth(final - 1), a)
+            across_time(nth(final - 1))
+
+        @pl.when(j == 1)
+        def _():
             to_twin(nth(final), a)
-
-        @pl.when(j < final)
-        def _():
-            across_time(nth(j + 1))
-
-        @pl.when(j == 1)
-        def _():
+            to_twin(nth(0), other)
             fill_partners(nth(final), a)
 
-        @pl.when(j >= 1)
-        def _():
-            to_twin(nth(j - 1), other)
-
-    to_twin(nth(final), other)
+        @pl.when(j == 2)
+        def _():
+            to_twin(nth(1), other)
+            across_time(nth(final))
+
+    to_twin(nth(final - 1), other)
 
     def arrive(j):
         q = nth(j)
@@ -350,6 +350,10 @@
             arrive(j)
 
         add_chunk(far, CHUNKS - 1 - j)
+
+        @pl.when(j == 1)
+        def _():
+            to_twin(nth(final), other)
 
     arrive(final)
     halo(0).wait_send()

time: 54.4 us -> 52.5 us (0.965)
  Pallas kernels: 54.3 us -> 52.4 us
    pallas_call x1, Pallas kernels: 49.7 us -> 47.8 us  [front(): pl.pallas_call(functools.partial(front_kernel, filters_t.shape[0], sizes,...]
where the time goes in v4:
time: 52.5 us; the launch traced here: 52.4 us
  Pallas kernels  52.4 us (100%)
    pallas_call x1, Pallas kernels, front(): pl.pallas_call(functools.partial(front_kernel, filters_t.shape[0], sizes,...  47.8 us
    pallas_call x1, Pallas kernels, rest(): pl.pallas_call(functools.partial(rest_kernel, scale, seg), out_shape=jax....  4.58 us

profile of v4, /device:TPU:0, one launch (start us, length us, event | category | flops | bytes accessed | tf_op | source)
XLA Modules:
  0.0 52.4 jit_solution(3064814449149075829)
XLA Ops:
  0.0 47.8 %front.1 = (bf16[8576,128]{1,0:T(8,128)(2,1)S(1)}, bf16[64,8576]{1,0:T(8,128)(2,1)S(1)}, f32[4160,256]{1,0:T(8,128)S(1)}) custom-call(f32[128,4096]{1,0:T(8,128)} %x_ref.1, f32[65,128]{1,0:T(8,128)} %bitcast.3, s32[1,128]{1,0:T(1,128)} %bitcast.4), custom_call_target="tpu_custom_call" | custom-call | tf_op jit(solution)/shard_map/front/pallas_call | solution.py:377
  47.8 4.6 %rest.1 = f32[129,64,128]{2,1,0:T(8,128)} custom-call(bf16[8576,128]{1,0:T(8,128)(2,1)S(1)} %get-tuple-element.8.w_ref, bf16[64,8576]{1,0:T(8,128)(2,1)S(1)} %get-tuple-element.9.xp_ref, f32[4160,256]{1,0:T(8,128)S(1)} %get-tuple-element.10.acc_ref), custom_call_target="tpu_custom_call" | custom-call | tf_op jit(solution)/shard_map/rest/pallas_call | solution.py:441

commit v5 on v4

--- a/solution.py
+++ b/solution.py
@@ -98,6 +98,30 @@
     rows = xp_ref.shape[0]
     for group, term in accumulated(w_ref, xp_ref, k0, depth, groups()):
         acc_ref[group[0] * rows : (group[-1] + 1) * rows, :] += term
+
+
+PAIRS = 128
+
+
+def weighted(x_ref, start, weights, count):
+    acc = None
+    for m, weight in enumerate(weights):
+        term = weight * x_ref[pl.ds(start + m, count), :]
+        acc = term if acc is None else acc + term
+    return acc
+
+
+def filtered_pairs(phases, start, f_ref, g_ref, taps, odd_sum, both):
+    even_x, odd_x, sum_x = phases
+    halves = taps // 2
+    odd_sum[...] = weighted(
+        odd_x, start, [f_ref[2 * m + 1 : 2 * m + 2, :] for m in range(halves)], PAIRS + 8
+    )
+    even = weighted(even_x, start, [f_ref[2 * m : 2 * m + 1, :] for m in range(halves + 1)], PAIRS)
+    both[pl.ds(0, PAIRS, stride=2), :] = even + odd_sum[0:PAIRS, :]
+    mixed = weighted(sum_x, start, [g_ref[m : m + 1, :] for m in range(halves + 1)], PAIRS)
+    both[pl.ds(1, PAIRS, stride=2), :] = mixed - (even + odd_sum[1 : PAIRS + 1, :])
+    return both[...]
 
 
 def routing_tables(src, block, rows, half, blocks, chan_dev, slot_most, wide):
@@ -135,7 +159,7 @@
 
 
 def front_kernel(taps, sizes, slot_most, x_ref, f_hbm, src_hbm, w_ref, xp_ref, acc_ref,
-                 f_ref, src_ref, x_v, xt, low, high, slot_ref, pick_ref, sel_ref,
+                 f_ref, src_ref, x_v, even_x, odd_x, sum_x, g_ref, odd_sum, both, xt, low, high, slot_ref, pick_ref, sel_ref,
                  x_sem, in_sem, halo_send, halo_recv, w_send, w_recv, slot_send, slot_recv):
     peers, lines, subs = sizes
     chans, seg = x_ref.shape
@@ -155,6 +179,14 @@
         pl.semaphore_signal(
             barrier, inc=1, device_id={"chan": lax.rem(z + step, lines)}, device_id_type=MESH
         )
+
+    def split(row):
+        here = pl.ds(pl.multiple_of(row // 2, 8), LANES // 2)
+        even = xt[pl.ds(row, LANES // 2, stride=2), :]
+        odd = xt[pl.ds(row + 1, LANES // 2, stride=2), :]
+        even_x[here, :] = even
+        odd_x[here, :] = odd
+        sum_x[here, :] = even + odd
 
     def x_copy(q):
         here = slice(q * width, (q + 1) * width)
@@ -175,6 +207,10 @@
     acc_ref[...] = jnp.zeros_like(acc_ref)
     for copy in small:
         copy.wait()
+    g_ref[0:1, :] = f_ref[0:1, :]
+    g_ref[1 : taps // 2 + 1, :] = (
+        f_ref[pl.ds(2, taps // 2, stride=2), :] + f_ref[pl.ds(1, taps // 2, stride=2), :]
+    )
 
     picker, select = routing_tables(
         src_ref[...], z * subs + s, rows, a, lines * subs, chans, slot_most, chans
@@ -261,14 +297,18 @@
         def _(b):
             t0 = pl.multiple_of(q * width + b * LANES, LANES)
             xt[pl.ds(t0 + EDGE, LANES), :] = x_v[:, pl.ds(t0, LANES)].T
+            split(t0 + EDGE)
 
     def whiten_chunk(q):
-        @pl.loop(0, width // TB)
+        @pl.loop(0, width // (2 * PAIRS))
         def _(b):
-            t0 = pl.multiple_of(q * width + b * TB, TB)
-            w_ref[pl.ds(pl.multiple_of(EDGE + a * seg + t0, TB), TB), :] = filtered(
-                xt, t0 + lead, f_ref, taps
-            ).astype(jnp.bfloat16)
+            t0 = pl.multiple_of(q * width + b * 2 * PAIRS, 2 * PAIRS)
+            start = pl.multiple_of((t0 + lead) // 2, 8)
+            w_ref[pl.ds(pl.multiple_of(EDGE + a * seg + t0, EDGE), 2 * PAIRS), :] = (
+                filtered_pairs(
+                    (even_x, odd_x, sum_x), start, f_ref, g_ref, taps, odd_sum, both
+                ).astype(jnp.bfloat16)
+            )
 
         slot_ref[a, z, s, :, columns(q)] = lax.dot_general(
             pick_ref[...], w_ref[pl.ds(place(a, q), width), :],
@@ -290,6 +330,8 @@
             halo(1).wait_recv()
             xt[0:EDGE, :] = jnp.where(a > 0, low[...], 0.0).T
             xt[seg + EDGE : seg + 2 * EDGE, :] = jnp.where(a < peers - 1, high[...], 0.0).T
+            split(0)
+            split(seg + EDGE)
 
         whiten_chunk(nth(j))
         launch(first(nth(j)))
@@ -387,6 +429,10 @@
             pltpu.VMEM(filters_t.shape, jnp.float32),
             pltpu.VMEM((1, sources.shape[0]), jnp.int32),
             pltpu.VMEM((chans, seg), jnp.float32),
+            *[pltpu.VMEM((seg // 2 + EDGE + 8, chans), jnp.float32)] * 3,
+            pltpu.VMEM((filters_t.shape[0] // 2 + 1, chans), jnp.float32),
+            pltpu.VMEM((PAIRS + 8, chans), jnp.float32),
+            pltpu.VMEM((2 * PAIRS, chans), jnp.float32),
             pltpu.VMEM((seg + 2 * EDGE, chans), jnp.float32),
             pltpu.VMEM((chans, EDGE), jnp.float32),
             pltpu.VMEM((chans, EDGE), jnp.float32),
@@ -541,7 +587,8 @@
     time_devs = lax.axis_size("tm")
     lines, subs = lax.axis_size("chan"), lax.axis_size("sub")
     scale = 1.0 / math.sqrt(seg_len * time_devs)
-    if time_devs == 2 and subs == 2 and chan_dev == LANES and seg_len % (CHUNKS * 256) == 0:
+    paired = filters.shape[1] % 32 == 1 and filters.shape[1] < 2 * LANES
+    if time_devs == 2 and subs == 2 and chan_dev == LANES and seg_len % (CHUNKS * 256) == 0 and paired:
         slot_most = min(chan_dev, sources.shape[0] // 8)
         w_full, partners, terms = front(
             traces, filters.T, sources, (time_devs, lines, subs), slot_most

time: 52.5 us -> 51.2 us (0.975)
  Pallas kernels: 52.4 us -> 51.1 us
    pallas_call x1, Pallas kernels: 47.8 us -> 46.5 us  [front(): pl.pallas_call(functools.partial(front_kernel, filters_t.shape[0], sizes,...]
where the time goes in v5:
time: 51.2 us; the launch traced here: 51.1 us
  Pallas kernels  51.1 us (100%)
    pallas_call x1, Pallas kernels, front(): pl.pallas_call(functools.partial(front_kernel, filters_t.shape[0], sizes,...  46.5 us
    pallas_call x1, Pallas kernels, rest(): pl.pallas_call(functools.partial(rest_kernel, scale, seg), out_shape=jax....  4.58 us

profile of v5, /device:TPU:0, one launch (start us, length us, event | category | flops | bytes accessed | tf_op | source)
XLA Modules:
  0.0 51.1 jit_solution(3332879689619068189)
XLA Ops:
  0.0 46.5 %front.1 = (bf16[8576,128]{1,0:T(8,128)(2,1)S(1)}, bf16[64,8576]{1,0:T(8,128)(2,1)S(1)}, f32[4160,256]{1,0:T(8,128)S(1)}) custom-call(f32[128,4096]{1,0:T(8,128)} %x_ref.1, f32[65,128]{1,0:T(8,128)} %bitcast.3, s32[1,128]{1,0:T(1,128)} %bitcast.4), custom_call_target="tpu_custom_call" | custom-call | tf_op jit(solution)/shard_map/front/pallas_call | solution.py:419
  46.5 4.6 %rest.1 = f32[129,64,128]{2,1,0:T(8,128)} custom-call(bf16[8576,128]{1,0:T(8,128)(2,1)S(1)} %get-tuple-element.8.w_ref, bf16[64,8576]{1,0:T(8,128)(2,1)S(1)} %get-tuple-element.9.xp_ref, f32[4160,256]{1,0:T(8,128)S(1)} %get-tuple-element.10.acc_ref), custom_call_target="tpu_custom_call" | custom-call | tf_op jit(solution)/shard_map/rest/pallas_call | solution.py:487

commit v6 on v5

--- a/solution.py
+++ b/solution.py
@@ -342,9 +342,6 @@
             to_twin(nth(j - 2), a)
 
     w_copy(nth(final), a).start()
-    across_time(nth(0))
-    to_twin(nth(final - 1), a)
-    across_time(nth(1))
 
     @pl.loop(0, 2)
     def _(j):
@@ -362,12 +359,15 @@
 
         @pl.when(j == 0)
         def _():
+            to_twin(nth(final - 1), a)
+            across_time(nth(0))
+            across_time(nth(1))
             fill_partners(nth(final - 1), a)
-            across_time(nth(final - 1))
 
         @pl.when(j == 1)
         def _():
             to_twin(nth(final), a)
+            across_time(nth(final - 1))
             to_twin(nth(0), other)
             fill_partners(nth(final), a)
 

time: 51.2 us -> 50.3 us (0.982); the launches traced: 51.1 us -> 49.4 us
  Pallas kernels: 51.1 us -> 49.4 us
    pallas_call x1, Pallas kernels: 46.5 us -> 44.9 us  [front(): pl.pallas_call(functools.partial(front_kernel, filters_t.shape[0], sizes,...]
where the time goes in v6:
time: 50.3 us; the launch traced here: 49.4 us
  Pallas kernels  49.4 us (98%)
    pallas_call x1, Pallas kernels, front(): pl.pallas_call(functools.partial(front_kernel, filters_t.shape[0], sizes,...  44.9 us
    pallas_call x1, Pallas kernels, rest(): pl.pallas_call(functools.partial(rest_kernel, scale, seg), out_shape=jax....  4.58 us

profile of v6, /device:TPU:0, one launch (start us, length us, event | category | flops | bytes accessed | tf_op | source)
XLA Modules:
  0.0 49.4 jit_solution(13452307780949946222)
XLA Ops:
  0.0 44.9 %front.1 = (bf16[8576,128]{1,0:T(8,128)(2,1)S(1)}, bf16[64,8576]{1,0:T(8,128)(2,1)S(1)}, f32[4160,256]{1,0:T(8,128)S(1)}) custom-call(f32[128,4096]{1,0:T(8,128)} %x_ref.1, f32[65,128]{1,0:T(8,128)} %bitcast.3, s32[1,128]{1,0:T(1,128)} %bitcast.4), custom_call_target="tpu_custom_call" | custom-call | tf_op jit(solution)/shard_map/front/pallas_call | solution.py:419
  44.9 4.6 %rest.1 = f32[129,64,128]{2,1,0:T(8,128)} custom-call(bf16[8576,128]{1,0:T(8,128)(2,1)S(1)} %get-tuple-element.8.w_ref, bf16[64,8576]{1,0:T(8,128)(2,1)S(1)} %get-tuple-element.9.xp_ref, f32[4160,256]{1,0:T(8,128)S(1)} %get-tuple-element.10.acc_ref), custom_call_target="tpu_custom_call" | custom-call | tf_op jit(solution)/shard_map/rest/pallas_call | solution.py:487
